TPU v7x, 512 devices: a whole 4x4x16 slice. The times are simulated.
512 devices in a mesh: rows: 32 (over z_lo, y), blk: 16 (over x, z_hi, core).
Axes of the slice: x: 4, y: 4, z: 16 (z_hi: 2, z_lo: 8; z = z_hi * 8 + z_lo), core: 2. Of those that a mesh axis runs over, the one named last changes fastest.
Arguments:
- features: bfloat16 [131072, 1024], P(('rows', 'blk')), may hold values from -6 to 6
- tiles: bfloat16 [512, 7, 256, 256], P(('rows', 'blk')), may hold values from -0.1875 to 0.1875
- tile_cols: int32 [512, 7], P(('rows', 'blk')), may hold values from 0 to 511, as said below
- tile_count: int32 [512], P(('rows', 'blk')), may hold values from 1 to 7
- weight: bfloat16 [1024, 1024], P(('rows', 'blk')), may hold values from -0.1875 to 0.1875
- cotangent: bfloat16 [131072, 1024], P(('rows', 'blk')), may hold values from -0.0625 to 0.0625
Outputs:
- output: bfloat16 [131072, 1024], P(('rows', 'blk'))
- weight_grad: float32 [1024, 1024], P(('rows', 'blk'))
Inputs may be any that keep to these rules, and one draw needn't show every extreme that they name: For each row block g, the first tile_count[g] entries of tile_cols[g] are distinct blocks of g's group of 16 blocks (blocks 16 * (g // 16) onward), each at most 3 positions from g around that group, g itself among them; the later entries are also blocks of that group and carry no tile.
All inputs are finite; a program needn't handle non-finite values.
Results may differ from a plain program's by a relative error of at most 0.0054.
Values may be sent and summed in bfloat16 or wider, within the bound.
A program may use at most 64 MiB of HBM per device.

v0:
```python
import jax
import jax.numpy as jnp
from jax import lax
from jax.sharding import PartitionSpec as P


def passed_along(value, axis, by):
    length = lax.axis_size(axis)
    return lax.ppermute(value, axis, [(i, (i + by) % length) for i in range(length)])


def local(features, tiles, tile_cols, tile_count, weight, cotangent):
    cycle_len = lax.axis_size("blk")
    position = lax.axis_index("blk")
    per_dev = tiles.shape[0]
    slot_total = tiles.shape[1]
    tile_side = tiles.shape[2]
    group_len = cycle_len * per_dev
    slot_ids = jnp.arange(slot_total, dtype=jnp.int32)
    columns = tile_cols % group_len

    def apply_panel(totals, panel_now, source):
        running = totals[0]
        in_use = slot_ids < tile_count[0]
        wanted = source * per_dev + 0
        match = jnp.logical_and(in_use, columns[0] == wanted)
        present = jnp.any(match)
        chosen_slot = jnp.sum(jnp.where(match, slot_ids, 0))
        chosen = lax.dynamic_index_in_dim(tiles[0], chosen_slot, 0, keepdims=False)
        rows_there = panel_now

        def multiply(chosen=chosen, rows_there=rows_there):
            return jnp.dot(chosen, rows_there, preferred_element_type=jnp.float32)

        def nothing():
            return jnp.zeros(running.shape, jnp.float32)

        running = running + lax.cond(present, multiply, nothing)
        updated = [running]
        return tuple(updated)

    empty = jnp.zeros((tile_side, features.shape[1]), jnp.float32)
    totals = tuple((empty for block_here in range(per_dev)))
    totals = apply_panel(totals, features, position)
    reach_blocks = min(3, (group_len - 1) // 2)
    reach_dev = (reach_blocks + per_dev - 1) // per_dev
    from_left = features
    from_right = features
    for offset in range(1, reach_dev + 1):
        from_left = passed_along(from_left, "blk", 1)
        totals = apply_panel(totals, from_left, (position - offset + cycle_len) % cycle_len)
        from_right = passed_along(from_right, "blk", -1)
        totals = apply_panel(totals, from_right, (position + offset) % cycle_len)
    aggregated = totals[0].astype(jnp.bfloat16)
    pre_act = lax.dot_general(
        aggregated,
        lax.all_gather(weight, ("rows", "blk"), axis=0, tiled=True),
        (((1,), (1,)), ((), ())),
        preferred_element_type=jnp.float32,
    )
    output = jax.nn.silu(pre_act).astype(jnp.bfloat16)
    sigmoid_y = jax.nn.sigmoid(pre_act)
    grad_pre = (
        cotangent.astype(jnp.float32) * sigmoid_y * (1.0 + pre_act * (1.0 - sigmoid_y))
    ).astype(jnp.bfloat16)
    weight_grad = lax.psum_scatter(
        lax.dot_general(
            grad_pre, aggregated, (((0,), (0,)), ((), ())), preferred_element_type=jnp.float32
        ),
        ("rows", "blk"),
        scatter_dimension=0,
        tiled=True,
    )
    return (output, weight_grad)


def solution(mesh):
    in_specs = (
        P(("rows", "blk"), None),
        P(("rows", "blk"), None, None, None),
        P(("rows", "blk"), None),
        P(("rows", "blk")),
        P(("rows", "blk"), None),
        P(("rows", "blk"), None),
    )
    out_specs = (P(("rows", "blk"), None), P(("rows", "blk"), None))
    return jax.shard_map(local, mesh=mesh, in_specs=in_specs, out_specs=out_specs, check_vma=False)
```

profile of v0, /device:TPU:2, one launch (start us, length us, event | category | flops | bytes accessed | tf_op | source)
XLA Modules:
  0.0 1387.6 jit_solution(14543954781679902342)
XLA Ops:
  7.9 1.9 collective-permute-start
  9.9 15.1 %collective-permute-start.1 = (bf16[256,1024]{1,0:T(8,128)(2,1)}, bf16[256,1024]{1,0:T(8,128)(2,1)S(1)}, u32[]{:S(2)}, u32[]{:S(2)}) collective-permute-start(bf16[256,1024]{1,0:T(8,128)(2,1)} %param.20), channel_id=1, source_target_pairs={{0,15},{1,0},{2,1},{3,2},{4,3},{5,4},{6,5},{7,6},{8,7},{9,8},{10,9... | collective-permute-start | bytes 1572872 | tf_op jit(solution)/shard_map/ppermute | solution.py:9
  25.0 5.4 collective-permute-done
  30.4 0.8 copy-done
  31.2 21.4 %collective-permute-start.2 = (bf16[256,1024]{1,0:T(8,128)(2,1)S(1)}, bf16[256,1024]{1,0:T(8,128)(2,1)}, u32[]{:S(2)}, u32[]{:S(2)}) collective-permute-start(bf16[256,1024]{1,0:T(8,128)(2,1)S(1)} %collective-permute-done), channel_id=1, source_target_pairs={{0,1},{1,2},{2,3},{3,4},{4,5},{5,6},{6,7},{7,8},{8,9},{9,10},{10,1... | collective-permute-start | bytes 1572872 | tf_op jit(solution)/shard_map/ppermute | solution.py:9
  52.6 6.6 collective-permute-done.1
  59.2 13.5 collective-permute-start.3
  72.7 6.4 collective-permute-done.2
  79.2 8.0 collective-permute-start.4
  87.7 13.8 collective-permute-start.5
  102.2 1.4 fusion.32
  103.5 0.8 fusion.33
  108.6 3.8 conditional.7
  111.0 1.4 fusion
  112.4 3.9 conditional.9
  115.1 1.2 fusion.8
  116.5 5.0 conditional.10
  119.1 2.4 fusion.12
  121.5 1.1 conditional.11
  121.5 1.1 broadcast.46
  122.6 1.1 conditional.12
  122.6 1.1 broadcast.47
  123.7 8.2 collective-permute-done.5
  132.0 1.1 conditional.13
  132.0 1.1 broadcast.48
  133.1 3.6 add_convert_fusion
  136.7 747.7 %all-gather.3.cloned.1.call-done = bf16[512,2,1024]{2,1,0:T(2,128)(2,1)} async-done(((bf16[1,2,1024]{2,1,0:T(2,128)(2,1)}), bf16[512,2,1024]{2,1,0:T(2,128)(2,1)}) %all-gather.3.cloned.1.call-update) | async-done | bytes 2097168 | tf_op jit(solution)/shard_map/all_gather | solution.py:57
  884.4 2.7 reshape.33
  887.2 1.6 multiply_convert_fusion.1
  888.8 3.0 fusion.28
  891.9 487.5 %all-reduce.3.cloned.1.call-done = f32[1024,1024]{1,0:T(8,128)} async-done(((f32[1024,1024]{1,0:T(8,128)}), f32[1024,1024]{1,0:T(8,128)}) %all-reduce.3.cloned.1.call-update) | async-done | bytes 4194320
  1379.4 1.4 constant_dynamic-slice_fusion
  (23 shorter events, 3.5 us)
Async XLA Ops:
  7.2 877.3 %all-gather.3.cloned.1.call-start = ((), (), s32[]{:S(2)}) async-start(), calls=%async_computation | async-start | bytes 2101248 | tf_op jit(solution)/shard_map/all_gather | solution.py:57
  7.9 1371.5 %all-reduce.3.cloned.1.call-start = ((), (), s32[]{:S(2)}) async-start(), calls=%async_computation.1 | async-start | bytes 8388608
  7.9 22.5 %collective-permute-start = (bf16[256,1024]{1,0:T(8,128)(2,1)}, bf16[256,1024]{1,0:T(8,128)(2,1)S(1)}, u32[]{:S(2)}, u32[]{:S(2)}) collective-permute-start(bf16[256,1024]{1,0:T(8,128)(2,1)} %param.20), channel_id=1, source_target_pairs={{0,1},{1,2},{2,3},{3,4},{4,5},{5,6},{6,7},{7,8},{8,9},{9,10},{10,1... | collective-permute-start | bytes 1572872 | tf_op jit(solution)/shard_map/ppermute | solution.py:9
  9.9 49.4 %collective-permute-start.1 = (bf16[256,1024]{1,0:T(8,128)(2,1)}, bf16[256,1024]{1,0:T(8,128)(2,1)S(1)}, u32[]{:S(2)}, u32[]{:S(2)}) collective-permute-start(bf16[256,1024]{1,0:T(8,128)(2,1)} %param.20), channel_id=1, source_target_pairs={{0,15},{1,0},{2,1},{3,2},{4,3},{5,4},{6,5},{7,6},{8,7},{9,8},{10,9... | collective-permute-start | bytes 1572872 | tf_op jit(solution)/shard_map/ppermute | solution.py:9
  30.4 0.8 copy-start
  31.2 47.9 %collective-permute-start.2 = (bf16[256,1024]{1,0:T(8,128)(2,1)S(1)}, bf16[256,1024]{1,0:T(8,128)(2,1)}, u32[]{:S(2)}, u32[]{:S(2)}) collective-permute-start(bf16[256,1024]{1,0:T(8,128)(2,1)S(1)} %collective-permute-done), channel_id=1, source_target_pairs={{0,1},{1,2},{2,3},{3,4},{4,5},{5,6},{6,7},{7,8},{8,9},{9,10},{10,1... | collective-permute-start | bytes 1572872 | tf_op jit(solution)/shard_map/ppermute | solution.py:9
  59.2 28.4 %collective-permute-start.3 = (bf16[256,1024]{1,0:T(8,128)(2,1)S(1)}, bf16[256,1024]{1,0:T(8,128)(2,1)}, u32[]{:S(2)}, u32[]{:S(2)}) collective-permute-start(bf16[256,1024]{1,0:T(8,128)(2,1)S(1)} %collective-permute-done.1), channel_id=1, source_target_pairs={{0,15},{1,0},{2,1},{3,2},{4,3},{5,4},{6,5},{7,6},{8,7},{9,8},{10,9... | collective-permute-start | bytes 1572872 | tf_op jit(solution)/shard_map/ppermute | solution.py:9
  79.2 43.5 %collective-permute-start.4 = (bf16[256,1024]{1,0:T(8,128)(2,1)}, bf16[256,1024]{1,0:T(8,128)(2,1)}, u32[]{:S(2)}, u32[]{:S(2)}) collective-permute-start(bf16[256,1024]{1,0:T(8,128)(2,1)} %collective-permute-done.2), channel_id=1, source_target_pairs={{0,1},{1,2},{2,3},{3,4},{4,5},{5,6},{6,7},{7,8},{8,9},{9,10},{10,1... | collective-permute-start | bytes 1572872 | tf_op jit(solution)/shard_map/ppermute | solution.py:9
  87.7 44.3 %collective-permute-start.5 = (bf16[256,1024]{1,0:T(8,128)(2,1)}, bf16[256,1024]{1,0:T(8,128)(2,1)}, u32[]{:S(2)}, u32[]{:S(2)}) collective-permute-start(bf16[256,1024]{1,0:T(8,128)(2,1)} %collective-permute-done.3), channel_id=1, source_target_pairs={{0,15},{1,0},{2,1},{3,2},{4,3},{5,4},{6,5},{7,6},{8,7},{9,8},{10,9... | collective-permute-start | bytes 1572872 | tf_op jit(solution)/shard_map/ppermute | solution.py:9
  136.7 750.5 %copy-start.1 = (bf16[256,1024]{1,0:T(8,128)(2,1)S(1)}, bf16[256,1024]{1,0:T(8,128)(2,1)}, u32[]{:S(2)}) copy-start(bf16[256,1024]{1,0:T(8,128)(2,1)} %add_convert_fusion) | copy-start | bytes 1572868
  887.2 1.6 copy-start.2
Sparse Core Ops, SparseCore 0:
  10.1 874.2 all-gather.2
  892.0 487.3 all-reduce.2
where the time goes:
time: 1390 us
  waiting for transfers between devices  1260 us (91%)
  starting transfers between devices  73.8 us (5%)
  between operations  19.2 us (1%)
    all_gather x1, waiting for transfers between devices, local(): lax.all_gather(weight, ('rows', 'blk'), axis=0, tiled=True)  748 us
    unnamed x3, waiting for transfers between devices  488 us
    ppermute x6, starting transfers between devices, passed_along(): lax.ppermute(value, axis, [(i, (i + by) % length) for i in range(length)])  73.7 us
  transfers between devices with their start and end apart: 8, of which 7 were waited for; matrix products, arithmetic and copies ran while one was open for 1% of the time, Pallas kernels for 0%

commit v1 on v0

--- a/solution.py
+++ b/solution.py
@@ -54,7 +54,12 @@
     aggregated = totals[0].astype(jnp.bfloat16)
     pre_act = lax.dot_general(
         aggregated,
-        lax.all_gather(weight, ("rows", "blk"), axis=0, tiled=True),
+        jnp.concatenate(
+            lax.all_to_all(
+                jnp.stack([weight] * lax.axis_size(("rows", "blk"))), ("rows", "blk"), 0, 0
+            ),
+            axis=0,
+        ),
         (((1,), (1,)), ((), ())),
         preferred_element_type=jnp.float32,
     )

time: 1390 us -> 828 us (0.60)
  waiting for transfers between devices: 1260 us -> 701 us
    all_gather x1 -> x0, waiting for transfers between devices: 748 us -> none  [local(): lax.all_gather(weight, ('rows', 'blk'), axis=0, tiled=True)]
    ppermute x6, waiting for transfers between devices: 27.2 us -> 177 us  [passed_along(): lax.ppermute(value, axis, [(i, (i + by) % length) for i in range(length)])]
    unnamed x3 -> x2, waiting for transfers between devices: 488 us -> 524 us
    ppermute x6, starting transfers between devices: 73.7 us -> 46.1 us  [passed_along(): lax.ppermute(value, axis, [(i, (i + by) % length) for i in range(length)])]
    all_to_all x0 -> x1, starting transfers between devices: none -> 23.3 us  [local(): lax.all_to_all(jnp.stack([weight] * lax.axis_size(('rows', 'blk'))), ('ro...]
  transfers between devices with their start and end apart: 8 -> 8, of which waited for: 7 -> 4; matrix products, arithmetic and copies ran while one was open for 1% -> 2% of each run, Pallas kernels for 0% -> 0%
where the time goes in v1:
time: 828 us; the launch traced here: 827 us
  waiting for transfers between devices  701 us (85%)
  starting transfers between devices  69.4 us (8%)
  between operations  19.2 us (2%)
  matrix products  12.5 us (2%)
  local copies, waits for them, and re-layouts  11.2 us (1%)
    unnamed x2, waiting for transfers between devices  524 us
    ppermute x6, waiting for transfers between devices, passed_along(): lax.ppermute(value, axis, [(i, (i + by) % length) for i in range(length)])  177 us
    ppermute x6, starting transfers between devices, passed_along(): lax.ppermute(value, axis, [(i, (i + by) % length) for i in range(length)])  46.1 us
    all_to_all x1, starting transfers between devices, local(): lax.all_to_all(jnp.stack([weight] * lax.axis_size(('rows', 'blk'))), ('ro...  23.3 us
  transfers between devices with their start and end apart: 8, of which 4 were waited for; matrix products, arithmetic and copies ran while one was open for 2% of the time, Pallas kernels for 0%

profile of v1, /device:TPU:2, one launch (start us, length us, event | category | flops | bytes accessed | tf_op | source)
XLA Modules:
  0.0 826.9 jit_solution(3725541395019141923)
XLA Ops:
  7.2 3.1 stack.2
  10.3 23.3 %all-to-all-start = ((bf16[512,2,1024]{2,1,0:T(2,128)(2,1)}), bf16[512,2,1024]{2,1,0:T(2,128)(2,1)S(1)}, u32[]{:S(2)}, u32[]{:S(2)}) async-start(bf16[512,2,1024]{2,1,0:T(2,128)(2,1)} %stack.2), calls=%async_computation | async-start | bytes 4194304 | tf_op jit(solution)/shard_map/all_to_all | solution.py:58
  33.7 2.0 collective-permute-start
  35.7 13.7 %collective-permute-start.1 = (bf16[256,1024]{1,0:T(8,128)(2,1)S(1)}, bf16[256,1024]{1,0:T(8,128)(2,1)S(1)}, u32[]{:S(2)}, u32[]{:S(2)}) collective-permute-start(bf16[256,1024]{1,0:T(8,128)(2,1)S(1)} %copy-done), channel_id=1, source_target_pairs={{0,15},{1,0},{2,1},{3,2},{4,3},{5,4},{6,5},{7,6},{8,7},{9,8},{10,9... | collective-permute-start | bytes 1572872 | tf_op jit(solution)/shard_map/ppermute | solution.py:9
  49.4 101.3 %collective-permute-done = bf16[256,1024]{1,0:T(8,128)(2,1)S(1)} collective-permute-done((bf16[256,1024]{1,0:T(8,128)(2,1)S(1)}, bf16[256,1024]{1,0:T(8,128)(2,1)S(1)}, u32[]{:S(2)}, u32[]{:S(2)}) %collective-permute-start) | collective-permute-done | bytes 524320 | tf_op jit(solution)/shard_map/ppermute | solution.py:9
  150.8 1.9 collective-permute-start.2
  152.7 13.3 %collective-permute-start.3 = (bf16[256,1024]{1,0:T(8,128)(2,1)S(1)}, bf16[256,1024]{1,0:T(8,128)(2,1)}, u32[]{:S(2)}, u32[]{:S(2)}) collective-permute-start(bf16[256,1024]{1,0:T(8,128)(2,1)S(1)} %collective-permute-done.1), channel_id=1, source_target_pairs={{0,15},{1,0},{2,1},{3,2},{4,3},{5,4},{6,5},{7,6},{8,7},{9,8},{10,9... | collective-permute-start | bytes 1572872 | tf_op jit(solution)/shard_map/ppermute | solution.py:9
  166.0 59.3 %collective-permute-done.2 = bf16[256,1024]{1,0:T(8,128)(2,1)} collective-permute-done((bf16[256,1024]{1,0:T(8,128)(2,1)S(1)}, bf16[256,1024]{1,0:T(8,128)(2,1)}, u32[]{:S(2)}, u32[]{:S(2)}) %collective-permute-start.2) | collective-permute-done | bytes 524320 | tf_op jit(solution)/shard_map/ppermute | solution.py:9
  225.3 1.9 collective-permute-start.4
  227.2 13.3 %collective-permute-start.5 = (bf16[256,1024]{1,0:T(8,128)(2,1)}, bf16[256,1024]{1,0:T(8,128)(2,1)}, u32[]{:S(2)}, u32[]{:S(2)}) collective-permute-start(bf16[256,1024]{1,0:T(8,128)(2,1)} %collective-permute-done.3), channel_id=1, source_target_pairs={{0,15},{1,0},{2,1},{3,2},{4,3},{5,4},{6,5},{7,6},{8,7},{9,8},{10,9... | collective-permute-start | bytes 1572872 | tf_op jit(solution)/shard_map/ppermute | solution.py:9
  241.9 0.8 fusion.33
  247.0 3.8 conditional.7
  249.4 1.4 fusion
  250.9 4.9 conditional.9
  253.4 2.4 fusion.8
  255.8 1.1 conditional.8
  255.8 1.1 broadcast.45
  256.9 5.0 conditional.10
  259.5 2.4 fusion.12
  261.9 1.1 conditional.11
  261.9 1.1 broadcast.48
  263.0 16.7 %collective-permute-done.4 = bf16[256,1024]{1,0:T(8,128)(2,1)} collective-permute-done((bf16[256,1024]{1,0:T(8,128)(2,1)}, bf16[256,1024]{1,0:T(8,128)(2,1)}, u32[]{:S(2)}, u32[]{:S(2)}) %collective-permute-start.4) | collective-permute-done | bytes 524320 | tf_op jit(solution)/shard_map/ppermute | solution.py:9
  279.8 1.1 conditional.12
  279.8 1.1 broadcast.49
  280.9 1.1 conditional.13
  280.9 1.1 broadcast.50
  282.0 4.3 add_convert_fusion
  286.3 2.2 reshape.37
  288.5 3.3 multiply_convert_fusion.1
  291.8 3.0 fusion.28
  294.8 523.9 %all-reduce.3.cloned.1.call-done = f32[1024,1024]{1,0:T(8,128)} async-done(((f32[1024,1024]{1,0:T(8,128)}), f32[1024,1024]{1,0:T(8,128)}) %all-reduce.3.cloned.1.call-update) | async-done | bytes 4194320
  818.7 1.4 constant_dynamic-slice_fusion
  (31 shorter events, 2.8 us)
Async XLA Ops:
  10.3 23.4 %copy-start = (bf16[256,1024]{1,0:T(8,128)(2,1)S(1)}, bf16[256,1024]{1,0:T(8,128)(2,1)}, u32[]{:S(2)}) copy-start(bf16[256,1024]{1,0:T(8,128)(2,1)} %param.20) | copy-start | bytes 1572868
  10.3 230.9 %copy-start.5 = (s32[1,7]{1,0:T(1,128)S(1)}, s32[1,7]{1,0:T(1,128)}, u32[]{:S(2)}) copy-start(s32[1,7]{1,0:T(1,128)} %param.22) | copy-start | bytes 88
  10.3 276.0 %all-to-all-start = ((bf16[512,2,1024]{2,1,0:T(2,128)(2,1)}), bf16[512,2,1024]{2,1,0:T(2,128)(2,1)S(1)}, u32[]{:S(2)}, u32[]{:S(2)}) async-start(bf16[512,2,1024]{2,1,0:T(2,128)(2,1)} %stack.2), calls=%async_computation | async-start | bytes 4194304 | tf_op jit(solution)/shard_map/all_to_all | solution.py:58
  33.6 785.1 %all-reduce.3.cloned.1.call-start = ((), (), s32[]{:S(2)}) async-start(), calls=%async_computation.1 | async-start | bytes 8388608
  33.7 117.1 %collective-permute-start = (bf16[256,1024]{1,0:T(8,128)(2,1)S(1)}, bf16[256,1024]{1,0:T(8,128)(2,1)S(1)}, u32[]{:S(2)}, u32[]{:S(2)}) collective-permute-start(bf16[256,1024]{1,0:T(8,128)(2,1)S(1)} %copy-done), channel_id=1, source_target_pairs={{0,1},{1,2},{2,3},{3,4},{4,5},{5,6},{6,7},{7,8},{8,9},{9,10},{10,1... | collective-permute-start | bytes 1572872 | tf_op jit(solution)/shard_map/ppermute | solution.py:9
  35.7 117.0 %collective-permute-start.1 = (bf16[256,1024]{1,0:T(8,128)(2,1)S(1)}, bf16[256,1024]{1,0:T(8,128)(2,1)S(1)}, u32[]{:S(2)}, u32[]{:S(2)}) collective-permute-start(bf16[256,1024]{1,0:T(8,128)(2,1)S(1)} %copy-done), channel_id=1, source_target_pairs={{0,15},{1,0},{2,1},{3,2},{4,3},{5,4},{6,5},{7,6},{8,7},{9,8},{10,9... | collective-permute-start | bytes 1572872 | tf_op jit(solution)/shard_map/ppermute | solution.py:9
  150.8 96.2 %copy-start.2 = (bf16[256,1024]{1,0:T(8,128)(2,1)}, bf16[256,1024]{1,0:T(8,128)(2,1)S(1)}, u32[]{:S(2)}) copy-start(bf16[256,1024]{1,0:T(8,128)(2,1)S(1)} %collective-permute-done) | copy-start | bytes 1572868
  150.8 74.5 %collective-permute-start.2 = (bf16[256,1024]{1,0:T(8,128)(2,1)S(1)}, bf16[256,1024]{1,0:T(8,128)(2,1)}, u32[]{:S(2)}, u32[]{:S(2)}) collective-permute-start(bf16[256,1024]{1,0:T(8,128)(2,1)S(1)} %collective-permute-done), channel_id=1, source_target_pairs={{0,1},{1,2},{2,3},{3,4},{4,5},{5,6},{6,7},{7,8},{8,9},{9,10},{10,1... | collective-permute-start | bytes 1572872 | tf_op jit(solution)/shard_map/ppermute | solution.py:9
  152.7 72.6 %copy-start.3 = (bf16[256,1024]{1,0:T(8,128)(2,1)}, bf16[256,1024]{1,0:T(8,128)(2,1)S(1)}, u32[]{:S(2)}) copy-start(bf16[256,1024]{1,0:T(8,128)(2,1)S(1)} %collective-permute-done.1) | copy-start | bytes 1572868
  152.7 74.5 %collective-permute-start.3 = (bf16[256,1024]{1,0:T(8,128)(2,1)S(1)}, bf16[256,1024]{1,0:T(8,128)(2,1)}, u32[]{:S(2)}, u32[]{:S(2)}) collective-permute-start(bf16[256,1024]{1,0:T(8,128)(2,1)S(1)} %collective-permute-done.1), channel_id=1, source_target_pairs={{0,15},{1,0},{2,1},{3,2},{4,3},{5,4},{6,5},{7,6},{8,7},{9,8},{10,9... | collective-permute-start | bytes 1572872 | tf_op jit(solution)/shard_map/ppermute | solution.py:9
  225.3 54.5 %collective-permute-start.4 = (bf16[256,1024]{1,0:T(8,128)(2,1)}, bf16[256,1024]{1,0:T(8,128)(2,1)}, u32[]{:S(2)}, u32[]{:S(2)}) collective-permute-start(bf16[256,1024]{1,0:T(8,128)(2,1)} %collective-permute-done.2), channel_id=1, source_target_pairs={{0,1},{1,2},{2,3},{3,4},{4,5},{5,6},{6,7},{7,8},{8,9},{9,10},{10,1... | collective-permute-start | bytes 1572872 | tf_op jit(solution)/shard_map/ppermute | solution.py:9
  227.2 53.7 %collective-permute-start.5 = (bf16[256,1024]{1,0:T(8,128)(2,1)}, bf16[256,1024]{1,0:T(8,128)(2,1)}, u32[]{:S(2)}, u32[]{:S(2)}) collective-permute-start(bf16[256,1024]{1,0:T(8,128)(2,1)} %collective-permute-done.3), channel_id=1, source_target_pairs={{0,15},{1,0},{2,1},{3,2},{4,3},{5,4},{6,5},{7,6},{8,7},{9,8},{10,9... | collective-permute-start | bytes 1572872 | tf_op jit(solution)/shard_map/ppermute | solution.py:9
  247.1 2.4 copy-start.1
  286.3 2.3 copy-start.4
  288.5 3.3 copy-start.6
Sparse Core Ops, SparseCore 0:
  294.9 523.7 all-reduce.2
